TPU v7x, 32 devices: a whole 2x2x4 slice. The times are simulated.
32 devices in a mesh: vel: 16 (over z, y, x), space: 2 (over core).
Axes of the slice: x: 2, y: 2, z: 4, core: 2. Of those that a mesh axis runs over, the one named last changes fastest.
Arguments:
- distribution: float32 [16384, 16, 128], P('vel', 'space'), may hold values from 0 to 11, as said below
- rate_class: int32 [16, 128], P('space'), may hold values from 0 to 7
- boundary_obstacle_indicator: int32 [16, 128], P('space'), may hold values 0 or 1
Outputs:
- field_out: float32 [16384, 16, 128], P('vel', 'space')
- latest_conserved_fields: float32 [5, 16, 128], P(None, 'space')
Inputs may be any that keep to these rules, and one draw needn't show every extreme that they name: `distribution`: every entry positive.
All inputs are finite; a program needn't handle non-finite values. No bound on the sum of `boundary_obstacle_indicator` on one device may be relied on, other than what follows from the above.
Results may differ from a plain program's by a relative error of at most 0.0003.
Values sent between devices are 32-bit elements; how exact they have to be, the bound alone decides.
A program may use at most 64 MiB of HBM per device.

v0:
```python
import jax
import jax.numpy as jnp
from jax import lax
from jax.sharding import PartitionSpec as P

VX = 32
VY = 32
VZ = 16
ITERS = 2
SWEEPS = 4
speed_edge = 5.0
marching_step_length = 0.1
momentum_thermal_ratio = 2.0 / 3.0
shear_power_law_index = 0.81
diffusivity = 1.0


def with_halo(value, sides, width):
    for axis, dim in sides:
        size, length = (lax.axis_size(axis), value.shape[dim])
        up = [(i, (i + 1) % size) for i in range(size)]
        down = [(j, i) for i, j in up]
        last = lax.slice_in_dim(value, length - width, length, axis=dim)
        leading = lax.slice_in_dim(value, 0, width, axis=dim)
        before = lax.ppermute(last, axis, up)
        after = lax.ppermute(leading, axis, down)
        value = jnp.concatenate([before, value, after], axis=dim)
    return value


def velocity_table(index):
    index_x = index % VX
    index_y = index // VX % VY
    index_z = index // (VX * VY)
    discrete_abscissa_xaxis = -speed_edge + (index_x.astype(jnp.float32) + 0.5) * (
        2.0 * speed_edge / VX
    )
    discrete_abscissa_yaxis = -speed_edge + (index_y.astype(jnp.float32) + 0.5) * (
        2.0 * speed_edge / VY
    )
    discrete_abscissa_zaxis = -speed_edge + (index_z.astype(jnp.float32) + 0.5) * (
        2.0 * speed_edge / VZ
    )
    return (discrete_abscissa_xaxis, discrete_abscissa_yaxis, discrete_abscissa_zaxis)


def moment_weights(discrete_abscissa_xaxis, discrete_abscissa_yaxis, discrete_abscissa_zaxis):
    square = (
        discrete_abscissa_xaxis * discrete_abscissa_xaxis
        + discrete_abscissa_yaxis * discrete_abscissa_yaxis
        + discrete_abscissa_zaxis * discrete_abscissa_zaxis
    )
    quadrature = (
        2.0
        * speed_edge
        / VX
        * (2.0 * speed_edge / VY)
        * (2.0 * speed_edge / VZ)
        / (2.0 * jnp.pi) ** 1.5
    )
    rows = [
        jnp.ones_like(discrete_abscissa_xaxis),
        discrete_abscissa_xaxis,
        discrete_abscissa_yaxis,
        discrete_abscissa_zaxis,
        square,
        discrete_abscissa_xaxis * discrete_abscissa_xaxis,
        discrete_abscissa_yaxis * discrete_abscissa_yaxis,
        discrete_abscissa_xaxis * discrete_abscissa_yaxis,
        discrete_abscissa_xaxis * discrete_abscissa_zaxis,
        discrete_abscissa_yaxis * discrete_abscissa_zaxis,
        discrete_abscissa_xaxis * square,
        discrete_abscissa_yaxis * square,
        discrete_abscissa_zaxis * square,
    ]
    return jnp.stack(rows) * quadrature


def conserved(moments):
    return jnp.stack([moments[0], moments[1], moments[2], moments[3], 0.5 * moments[4]])


def heat_flux(moments):
    mass = moments[0]
    flow_x = moments[1] / mass
    flow_y = moments[2] / mass
    flow_z = moments[3] / mass
    p_xx = moments[5]
    p_yy = moments[6]
    p_zz = moments[4] - moments[5] - moments[6]
    p_xy = moments[7]
    p_xz = moments[8]
    p_yz = moments[9]
    flow_sq = flow_x * flow_x + flow_y * flow_y + flow_z * flow_z
    heat_x = 0.5 * (
        moments[10]
        - 2.0 * (flow_x * p_xx + flow_y * p_xy + flow_z * p_xz)
        - flow_x * moments[4]
        + 2.0 * mass * flow_sq * flow_x
    )
    heat_y = 0.5 * (
        moments[11]
        - 2.0 * (flow_x * p_xy + flow_y * p_yy + flow_z * p_yz)
        - flow_y * moments[4]
        + 2.0 * mass * flow_sq * flow_y
    )
    heat_z = 0.5 * (
        moments[12]
        - 2.0 * (flow_x * p_xz + flow_y * p_yz + flow_z * p_zz)
        - flow_z * moments[4]
        + 2.0 * mass * flow_sq * flow_z
    )
    return jnp.stack([heat_x, heat_y, heat_z])


def transport(field, courant_x, courant_y):
    from_left = jnp.roll(field, 1, 2)
    from_right = jnp.roll(field, -1, 2)
    term_y = jnp.where(
        courant_y > 0, courant_y * (field - from_left), courant_y * (from_right - field)
    )
    padded = with_halo(field, (("space", 1),), 1)
    term_x = jnp.where(
        courant_x > 0, courant_x * (field - padded[:, :-2]), courant_x * (padded[:, 2:] - field)
    )
    return field - term_x - term_y


def diffuse(source):
    margin = with_halo(source, (("space", 1),), SWEEPS)
    iterate = margin
    for sweep_index in range(SWEEPS):
        inner = iterate[:, 1:-1]
        beside = iterate[:, :-2] + iterate[:, 2:] + jnp.roll(inner, 1, 2) + jnp.roll(inner, -1, 2)
        margin_edge = sweep_index + 1
        iterate = (
            margin[:, margin_edge : margin.shape[1] - margin_edge] + diffusivity * beside
        ) / (1.0 + 4.0 * diffusivity)
    return iterate


def collision_update_piece(
    convected_fields,
    discrete_abscissa_xaxis,
    discrete_abscissa_yaxis,
    discrete_abscissa_zaxis,
    particle_concentration,
    mean_drift_velocity,
    kinetic_thermal_level,
    energy_flux_components,
    collision_frequency,
    obstacle_indicators,
):
    diff_x = discrete_abscissa_xaxis - mean_drift_velocity[0]
    diff_y = discrete_abscissa_yaxis - mean_drift_velocity[1]
    diff_z = discrete_abscissa_zaxis - mean_drift_velocity[2]
    quadratic_deviation = diff_x * diff_x + diff_y * diff_y + diff_z * diff_z
    prefactor_amplitude = particle_concentration * kinetic_thermal_level ** (-1.5)
    local_gaussian_population = prefactor_amplitude * jnp.exp(
        -0.5 * quadratic_deviation / kinetic_thermal_level
    )
    skewed_correction_multiplier = (1.0 - momentum_thermal_ratio) / (
        5.0 * particle_concentration * kinetic_thermal_level * kinetic_thermal_level
    )
    projected_energy_flux = (
        diff_x * energy_flux_components[0]
        + diff_y * energy_flux_components[1]
        + diff_z * energy_flux_components[2]
    )
    goal_population = local_gaussian_population * (
        1.0
        + skewed_correction_multiplier
        * projected_energy_flux
        * (quadratic_deviation / kinetic_thermal_level - 5.0)
    )
    wall_state = particle_concentration * jnp.exp(
        -0.5
        * (
            discrete_abscissa_xaxis * discrete_abscissa_xaxis
            + discrete_abscissa_yaxis * discrete_abscissa_yaxis
            + discrete_abscissa_zaxis * discrete_abscissa_zaxis
        )
    )
    relaxed = convected_fields + collision_frequency * (goal_population - convected_fields)
    return jnp.where(obstacle_indicators > 0, wall_state, relaxed)


def per_device(distribution, rate_class, boundary_obstacle_indicator):
    vel_count, row_count, col_count = distribution.shape
    index = lax.axis_index("vel") * vel_count + jnp.arange(vel_count, dtype=jnp.int32)
    discrete_abscissa_xaxis, discrete_abscissa_yaxis, discrete_abscissa_zaxis = velocity_table(
        index
    )
    weights = moment_weights(
        discrete_abscissa_xaxis, discrete_abscissa_yaxis, discrete_abscissa_zaxis
    )
    column_x = discrete_abscissa_xaxis[:, None, None]
    column_y = discrete_abscissa_yaxis[:, None, None]
    column_z = discrete_abscissa_zaxis[:, None, None]
    courant_x = marching_step_length * column_x
    courant_y = marching_step_length * column_y
    reference_collision_freq = 0.5 * jnp.exp2(rate_class.astype(jnp.float32))
    field = distribution
    latest_conserved_fields = jnp.zeros((5, row_count, col_count), jnp.float32)
    for step_index in range(ITERS):
        convected_fields = transport(field, courant_x, courant_y)
        partial_value = jnp.dot(
            weights,
            convected_fields.reshape(vel_count, row_count * col_count),
            precision=lax.Precision.HIGHEST,
            preferred_element_type=jnp.float32,
        )
        moments = lax.psum(partial_value, "vel")
        source = conserved(moments)
        energy_flux_components = heat_flux(moments)
        source = source.reshape(5, row_count, col_count)
        energy_flux_components = energy_flux_components.reshape(3, row_count, col_count)
        latest_conserved_fields = diffuse(source)
        particle_concentration = latest_conserved_fields[0]
        mean_drift_velocity = latest_conserved_fields[1:4] / particle_concentration
        kinetic_thermal_level = (
            2.0 * latest_conserved_fields[4] / particle_concentration
            - (
                mean_drift_velocity[0] * mean_drift_velocity[0]
                + mean_drift_velocity[1] * mean_drift_velocity[1]
                + mean_drift_velocity[2] * mean_drift_velocity[2]
            )
        ) / 3.0
        collision_frequency = 1.0 - jnp.exp(
            -marching_step_length
            * reference_collision_freq
            * particle_concentration
            * kinetic_thermal_level ** (1.0 - shear_power_law_index)
        )
        field = collision_update_piece(
            convected_fields,
            column_x,
            column_y,
            column_z,
            particle_concentration,
            mean_drift_velocity,
            kinetic_thermal_level,
            energy_flux_components,
            collision_frequency,
            boundary_obstacle_indicator,
        )
    return (field, latest_conserved_fields)


def solution(mesh):
    placed = (P("vel", "space", None), P("space", None), P("space", None))
    return jax.shard_map(
        per_device,
        mesh=mesh,
        in_specs=placed,
        out_specs=(P("vel", "space", None), P(None, "space", None)),
        check_vma=False,
    )
```

profile of v0, /device:TPU:0, one launch (start us, length us, event | category | flops | bytes accessed | tf_op | source)
XLA Modules:
  0.0 239.6 jit_solution(17886712523408883976)
XLA Ops:
  0.6 4.2 %fusion.177 = (f32[1024,1,128]{2,1,0:T(1,128)S(1)}, f32[1024,1,128]{2,1,0:T(1,128)S(1)}) fusion(f32[1024,8,128]{2,1,0:T(8,128)} %param.3), kind=kLoop, calls=%fused_computation.291 | loop fusion | bytes 2097152 | tf_op jit(solution)/shard_map/slice | solution.py:23
  4.8 0.6 collective-permute-start.1
  5.4 0.1 collective-permute-start
  5.5 0.1 multiply_add_fusion
  5.6 0.1 fusion.164
  5.7 0.1 fusion.166
  5.8 0.1 fusion.170
  6.1 5.4 %copy.27 = f32[1024,8,128]{0,2,1:T(8,128)} copy(f32[1024,8,128]{2,1,0:T(8,128)} %param.3) | data formatting | bytes 8388608 | tf_op args[0]
  11.4 1.1 fusion.176
  12.5 0.1 stack.16
  12.6 8.7 %fusion.175 = (f32[1024,8,127]{0,2,1:T(8,128)}, f32[1024,8,127]{0,2,1:T(8,128)}) fusion(f32[1024,8,128]{0,2,1:T(8,128)} %copy.27), kind=kLoop, calls=%fused_computation.289 | loop fusion | bytes 16646144 | tf_op jit(solution)/shard_map/jit(_roll_static)/slice | solution.py:118
  21.4 0.2 copy.25
  21.6 0.2 copy.20
  21.8 8.6 %fusion.47 = f32[1024,8,128]{0,2,1:T(8,128)S(1)} fusion(f32[1024,8,128]{0,2,1:T(8,128)} %copy.27, f32[1024,1,128]{0,2,1:T(8,128)S(1)} %copy.25, f32[1024,1,128]{0,2,1:T(8,128)S(1)} %copy.20, f32[1024,8,127]{0,2,1:T(8,128)} %get-tuple-element.17, f32[1024,8,1]{0,2,1:T(1,128)S(1)} %get-tuple-element.19, f32[1024,8,1]{0,2,1:T(1,128)S(1)} %get-tuple-element.18, ...), kind=kLoop, calls=%fused_computation.62 | loop fusion | flops 16777216 | bytes 17836032 | tf_op jit(solution)/shard_map/sub | solution.py:126
  30.4 2.0 copy-done.2
  32.4 3.6 %fusion.58 = f32[13,1024]{1,0:T(8,128)S(1)} fusion(f32[1024,1024]{0,1:T(8,128)S(1)} %bitcast.95, f32[13,1024]{1,0:T(8,128)S(1)} %stack.16), kind=kOutput, calls=%fused_computation.78 | convolution fusion | flops 163591168 | bytes 4300800 | tf_op jit(solution)/shard_map/dot_general | solution.py:207
  36.0 78.6 %psum.14 = f32[13,1024]{1,0:T(8,128)S(1)} all-reduce(f32[13,1024]{1,0:T(8,128)S(1)} %fusion.58), channel_id=1, replica_groups=mesh['vel'=16,'space'=2] {'vel'}, use_global_device_ids=true, to_apply=%region_0.1 | all-reduce | flops 13312 | bytes 106496 | tf_op jit(solution)/shard_map/psum | solution.py:213
  114.8 0.5 collective-permute-start.3
  115.3 0.6 collective-permute-done.2
  115.9 0.2 collective-permute-done.3
  116.1 0.1 fusion.193
  116.3 0.1 fusion.83
  116.5 0.1 fusion.79
  116.6 0.1 fusion.188
  116.8 0.1 fusion.75
  117.0 0.1 fusion.89
  117.2 7.4 %fusion.11 = f32[1024,8,128]{0,2,1:T(8,128)S(1)} fusion(f32[1024,8,128]{0,2,1:T(8,128)} %copy-done.2, f32[8,128]{1,0:T(8,128)S(1)} %bitcast.117, f32[8,128]{1,0:T(8,128)S(1)} %bitcast.115, f32[8,128]{1,0:T(8,128)S(1)} %bitcast.114, f32[8,128]{1,0:T(8,128)S(1)} %fusion.113, f32[8,128]{1,0:T(8,128)S(1)} %bitcast.111, f32[8,128]{1,0:T(8,128)S(1)} %get-tuple-element.71, ...), kind=kLoop, calls=%fused_computation.23 | loop fusion | flops 28311552 | bytes 8451072 | tf_op jit(solution)/shard_map/jit(_where)/select_n | solution.py:185
  124.7 1.9 copy-done
  126.7 0.2 copy.34
  126.9 0.2 copy.36
  127.1 0.4 collective-permute-start.5
  127.5 0.2 collective-permute-start.4
  127.7 8.7 %fusion.172 = (f32[1024,8,127]{0,2,1:T(8,128)}, f32[1024,8,127]{0,2,1:T(8,128)}) fusion(f32[1024,8,128]{0,2,1:T(8,128)} %copy-done), kind=kLoop, calls=%fused_computation.286 | loop fusion | bytes 16646144 | tf_op jit(solution)/shard_map/jit(_roll_static)/slice | solution.py:118
  136.5 0.2 copy.37
  136.7 0.2 copy.35
  136.9 8.6 %fusion.40 = f32[1024,8,128]{0,2,1:T(8,128)S(1)} fusion(f32[1024,8,128]{0,2,1:T(8,128)} %copy-done, f32[1024,1,128]{0,2,1:T(8,128)S(1)} %copy.37, f32[1024,1,128]{0,2,1:T(8,128)S(1)} %copy.35, f32[1024,8,127]{0,2,1:T(8,128)} %get-tuple-element.11, f32[1024,8,1]{0,2,1:T(1,128)S(1)} %get-tuple-element.13, f32[1024,8,1]{0,2,1:T(1,128)S(1)} %get-tuple-element.12, ...), kind=kLoop, calls=%fused_computation.53 | loop fusion | flops 16777216 | bytes 17836032 | tf_op jit(solution)/shard_map/sub | solution.py:126
  145.5 2.0 copy-done.1
  147.5 3.6 %fusion.56 = f32[13,1024]{1,0:T(8,128)S(1)} fusion(f32[1024,1024]{0,1:T(8,128)S(1)} %bitcast.94, f32[13,1024]{1,0:T(8,128)S(1)} %stack.16), kind=kOutput, calls=%fused_computation.76 | convolution fusion | flops 163591168 | bytes 4300800 | tf_op jit(solution)/shard_map/dot_general | solution.py:207
  151.1 71.8 %psum.15 = f32[13,1024]{1,0:T(8,128)S(1)} all-reduce(f32[13,1024]{1,0:T(8,128)S(1)} %fusion.56), channel_id=1, replica_groups=mesh['vel'=16,'space'=2] {'vel'}, use_global_device_ids=true, to_apply=%region_1.2 | all-reduce | flops 13312 | bytes 106496 | tf_op jit(solution)/shard_map/psum | solution.py:213
  223.0 0.5 collective-permute-start.7
  223.6 0.6 collective-permute-done.6
  224.2 0.2 collective-permute-done.7
  224.5 0.1 fusion.71
  224.8 0.1 fusion.67
  225.0 0.1 fusion.63
  225.3 0.1 fusion.87
  225.5 8.8 %fusion.29 = f32[1024,8,128]{0,2,1:T(8,128)} fusion(f32[1024,8,128]{0,2,1:T(8,128)} %copy-done.1, f32[8,128]{1,0:T(8,128)S(1)} %bitcast.116, f32[8,128]{1,0:T(8,128)S(1)} %bitcast.113, f32[8,128]{1,0:T(8,128)S(1)} %bitcast.112, f32[8,128]{1,0:T(8,128)S(1)} %fusion.115, f32[8,128]{1,0:T(8,128)S(1)} %bitcast.110, f32[8,128]{1,0:T(8,128)S(1)} %get-tuple-element.68, ...), kind=kLoop, calls=%fused_computation.41 | loop fusion | flops 28311552 | bytes 8451072 | tf_op jit(solution)/shard_map/jit(_where)/select_n | solution.py:185
  234.3 5.4 %copy.38 = f32[1024,8,128]{2,1,0:T(8,128)} copy(f32[1024,8,128]{0,2,1:T(8,128)} %fusion.29) | data formatting | bytes 8388608
  (61 shorter events, 2.0 us)
Async XLA Ops:
  4.8 16.6 %collective-permute-start.1 = (f32[1024,1,128]{2,0,1:T(8,128)S(1)}, f32[1024,1,128]{2,0,1:T(8,128)S(1)}, u32[]{:S(2)}, u32[]{:S(2)}) collective-permute-start(f32[1024,1,128]{2,0,1:T(8,128)S(1)} %bitcast.97), channel_id=1, source_target_pairs={{1,0},{0,1},{3,2},{2,3},{5,4},{4,5},{7,6},{6,7},{9,8},{8,9},{11,10... | collective-permute-start | bytes 1572872 | tf_op jit(solution)/shard_map/ppermute | solution.py:26
  5.4 16.2 %collective-permute-start = (f32[1024,1,128]{2,0,1:T(8,128)S(1)}, f32[1024,1,128]{2,0,1:T(8,128)S(1)}, u32[]{:S(2)}, u32[]{:S(2)}) collective-permute-start(f32[1024,1,128]{2,0,1:T(8,128)S(1)} %bitcast.96), channel_id=1, source_target_pairs={{0,1},{1,0},{2,3},{3,2},{4,5},{5,4},{6,7},{7,6},{8,9},{9,8},{10,11... | collective-permute-start | bytes 1572872 | tf_op jit(solution)/shard_map/ppermute | solution.py:25
  6.1 5.4 %copy-start.5 = (s32[8,128]{1,0:T(8,128)S(1)}, s32[8,128]{1,0:T(8,128)}, u32[]{:S(2)}) copy-start(s32[8,128]{1,0:T(8,128)} %param.5) | copy-start | bytes 12292
  30.4 2.0 copy-start.2
  30.4 86.7 %copy-start.4 = (s32[8,128]{1,0:T(8,128)S(1)}, s32[8,128]{1,0:T(8,128)}, u32[]{:S(2)}) copy-start(s32[8,128]{1,0:T(8,128)} %param.4) | copy-start | bytes 12292
  114.7 1.2 collective-permute-start.2
  114.8 1.3 collective-permute-start.3
  124.6 2.0 copy-start
  127.1 9.3 %collective-permute-start.5 = (f32[1024,1,128]{2,0,1:T(8,128)S(1)}, f32[1024,1,128]{2,0,1:T(8,128)S(1)}, u32[]{:S(2)}, u32[]{:S(2)}) collective-permute-start(f32[1024,1,128]{2,0,1:T(8,128)S(1)} %copy.36), channel_id=1, source_target_pairs={{1,0},{0,1},{3,2},{2,3},{5,4},{4,5},{7,6},{6,7},{9,8},{8,9},{11,10... | collective-permute-start | bytes 1572872 | tf_op jit(solution)/shard_map/ppermute | solution.py:26
  127.5 9.1 %collective-permute-start.4 = (f32[1024,1,128]{2,0,1:T(8,128)S(1)}, f32[1024,1,128]{2,0,1:T(8,128)S(1)}, u32[]{:S(2)}, u32[]{:S(2)}) collective-permute-start(f32[1024,1,128]{2,0,1:T(8,128)S(1)} %copy.34), channel_id=1, source_target_pairs={{0,1},{1,0},{2,3},{3,2},{4,5},{5,4},{6,7},{7,6},{8,9},{9,8},{10,11... | collective-permute-start | bytes 1572872 | tf_op jit(solution)/shard_map/ppermute | solution.py:25
  145.5 2.0 copy-start.1
  222.9 1.2 collective-permute-start.6
  223.0 1.3 collective-permute-start.7
  225.4 8.9 %copy-start.3 = (f32[5,8,128]{2,1,0:T(8,128)}, f32[5,8,128]{2,1,0:T(8,128)S(1)}, u32[]{:S(2)}) copy-start(f32[5,8,128]{2,1,0:T(8,128)S(1)} %fusion.87) | copy-start | bytes 61444
where the time goes:
time: 240 us
  blocking collectives  150 us (62%)
  local copies, waits for them, and re-layouts  42.1 us (18%)
  other arithmetic  35.1 us (15%)
  matrix products  7.12 us (3%)
    psum x2, blocking collectives, per_device(): moments = lax.psum(partial_value, 'vel')  150 us
    slice x4, local copies, waits for them, and re-layouts, transport(): from_right = jnp.roll(field, -1, 2)  18.6 us
    sub x2, other arithmetic, transport(): return field - term_x - term_y  17.2 us
    unnamed x18, local copies, waits for them, and re-layouts  16.7 us
    select_n x2, other arithmetic, collision_update_piece(): return jnp.where(obstacle_indicators > 0, wall_state, relaxed)  16.2 us
    dot_general x2, matrix products, per_device(): jnp.dot(weights, convected_fields.reshape(vel_count, row_count * col_coun...  7.12 us
  transfers between devices with their start and end apart: 8, of which 4 were waited for; matrix products, arithmetic and copies ran while one was open for 10% of the time, Pallas kernels for 0%

commit v1 on v0

--- a/solution.py
+++ b/solution.py
@@ -210,7 +210,11 @@
             precision=lax.Precision.HIGHEST,
             preferred_element_type=jnp.float32,
         )
-        moments = lax.psum(partial_value, "vel")
+        moments = partial_value
+        devs = lax.axis_size("vel")
+        for dev in [[(t, t ^ w) for t in range(devs)] for w in (1, 2, 4, 8, 16) if w < devs]:
+            all_rows = lax.ppermute(moments, axis_name="vel", perm=dev)
+            moments = moments + all_rows
         source = conserved(moments)
         energy_flux_components = heat_flux(moments)
         source = source.reshape(5, row_count, col_count)

time: 240 us -> 119 us (0.50)
  blocking collectives: 150 us -> 0 us
  waiting for transfers between devices: 1.54 us -> 21.4 us
  starting transfers between devices: 2.35 us -> 20.9 us
  other arithmetic: 35.1 us -> 30.2 us
  local copies, waits for them, and re-layouts: 42.1 us -> 38.1 us
    psum x2 -> x0, blocking collectives: 150 us -> none  [per_device(): moments = lax.psum(partial_value, 'vel')]
    ppermute x0 -> x8, waiting for transfers between devices: none -> 19.9 us  [per_device(): all_rows = lax.ppermute(moments, axis_name='vel', perm=dev)]
    ppermute x0 -> x8, starting transfers between devices: none -> 18.6 us  [per_device(): all_rows = lax.ppermute(moments, axis_name='vel', perm=dev)]
    select_n x2, other arithmetic: 16.2 us -> 11 us  [collision_update_piece(): return jnp.where(obstacle_indicators > 0, wall_state, relaxed)]
    unnamed x18 -> x14, local copies, waits for them, and re-layouts: 16.7 us -> 12.7 us
  transfers between devices with their start and end apart: 8 -> 16, of which waited for: 4 -> 12; matrix products, arithmetic and copies ran while one was open for 10% -> 21% of each run, Pallas kernels for 0% -> 0%
where the time goes in v1:
time: 119 us
  local copies, waits for them, and re-layouts  38.1 us (32%)
  other arithmetic  30.2 us (25%)
  waiting for transfers between devices  21.4 us (18%)
  starting transfers between devices  20.9 us (18%)
  matrix products  7.13 us (6%)
    ppermute x8, waiting for transfers between devices, per_device(): all_rows = lax.ppermute(moments, axis_name='vel', perm=dev)  19.9 us
    slice x4, local copies, waits for them, and re-layouts, transport(): from_right = jnp.roll(field, -1, 2)  18.6 us
    ppermute x8, starting transfers between devices, per_device(): all_rows = lax.ppermute(moments, axis_name='vel', perm=dev)  18.6 us
    sub x2, other arithmetic, transport(): return field - term_x - term_y  17.4 us
    unnamed x14, local copies, waits for them, and re-layouts  12.7 us
    select_n x2, other arithmetic, collision_update_piece(): return jnp.where(obstacle_indicators > 0, wall_state, relaxed)  11 us
    dot_general x2, matrix products, per_device(): jnp.dot(weights, convected_fields.reshape(vel_count, row_count * col_coun...  7.13 us
    slice x3, local copies, waits for them, and re-layouts, with_halo(): last = lax.slice_in_dim(value, length - width, length, axis=dim)  4.45 us
  transfers between devices with their start and end apart: 16, of which 12 were waited for; matrix products, arithmetic and copies ran while one was open for 21% of the time, Pallas kernels for 0%

profile of v1, /device:TPU:0, one launch (start us, length us, event | category | flops | bytes accessed | tf_op | source)
XLA Modules:
  0.0 118.8 jit_solution(4816543170673697770)
XLA Ops:
  0.6 4.2 %fusion.177 = (f32[1024,1,128]{2,1,0:T(1,128)S(1)}, f32[1024,1,128]{2,1,0:T(1,128)S(1)}) fusion(f32[1024,8,128]{2,1,0:T(8,128)} %param.3), kind=kLoop, calls=%fused_computation.291 | loop fusion | bytes 2097152 | tf_op jit(solution)/shard_map/slice | solution.py:23
  4.8 0.6 collective-permute-start.1
  6.0 5.4 %copy.27 = f32[1024,8,128]{0,2,1:T(8,128)} copy(f32[1024,8,128]{2,1,0:T(8,128)} %param.3) | data formatting | bytes 8388608 | tf_op args[0]
  11.4 1.1 fusion.176
  12.5 0.1 stack.16
  12.6 8.7 %fusion.175 = (f32[1024,8,127]{0,2,1:T(8,128)}, f32[1024,8,127]{0,2,1:T(8,128)}) fusion(f32[1024,8,128]{0,2,1:T(8,128)} %copy.27), kind=kLoop, calls=%fused_computation.289 | loop fusion | bytes 16646144 | tf_op jit(solution)/shard_map/jit(_roll_static)/slice | solution.py:118
  21.3 0.2 copy.25
  21.6 0.2 copy.20
  21.8 8.6 %fusion.47 = f32[1024,8,128]{0,2,1:T(8,128)S(1)} fusion(f32[1024,8,128]{0,2,1:T(8,128)} %copy.27, f32[1024,1,128]{0,2,1:T(8,128)S(1)} %copy.25, f32[1024,1,128]{0,2,1:T(8,128)S(1)} %copy.20, f32[1024,8,127]{0,2,1:T(8,128)} %get-tuple-element.17, f32[1024,8,1]{0,2,1:T(1,128)S(1)} %get-tuple-element.19, f32[1024,8,1]{0,2,1:T(1,128)S(1)} %get-tuple-element.18, ...), kind=kLoop, calls=%fused_computation.62 | loop fusion | flops 16777216 | bytes 17836032 | tf_op jit(solution)/shard_map/sub | solution.py:126
  30.4 3.6 %fusion.58 = f32[13,1024]{1,0:T(8,128)S(1)} fusion(f32[1024,1024]{0,1:T(8,128)S(1)} %bitcast.95, f32[13,1024]{1,0:T(8,128)S(1)} %stack.16), kind=kOutput, calls=%fused_computation.78 | convolution fusion | flops 163591168 | bytes 4300800 | tf_op jit(solution)/shard_map/dot_general | solution.py:207
  34.0 2.9 %collective-permute-start.2 = (f32[13,1024]{1,0:T(8,128)S(1)}, f32[13,1024]{1,0:T(8,128)S(1)}, u32[]{:S(2)}, u32[]{:S(2)}) collective-permute-start(f32[13,1024]{1,0:T(8,128)S(1)} %fusion.58), channel_id=1, source_target_pairs={{0,2},{2,0},{4,6},{6,4},{8,10},{10,8},{12,14},{14,12},{16,18},{18,... | collective-permute-start | bytes 159752 | tf_op jit(solution)/shard_map/ppermute | solution.py:216
  36.9 2.3 %collective-permute-done.2 = f32[13,1024]{1,0:T(8,128)S(1)} collective-permute-done((f32[13,1024]{1,0:T(8,128)S(1)}, f32[13,1024]{1,0:T(8,128)S(1)}, u32[]{:S(2)}, u32[]{:S(2)}) %collective-permute-start.2) | collective-permute-done | bytes 53280 | tf_op jit(solution)/shard_map/ppermute | solution.py:216
  39.3 2.0 %collective-permute-start.3 = (f32[13,1024]{1,0:T(8,128)S(1)}, f32[13,1024]{1,0:T(8,128)S(1)}, u32[]{:S(2)}, u32[]{:S(2)}) collective-permute-start(f32[13,1024]{1,0:T(8,128)S(1)} %add.950), channel_id=1, source_target_pairs={{0,4},{2,6},{4,0},{6,2},{8,12},{10,14},{12,8},{14,10},{16,20},{18,... | collective-permute-start | bytes 159752 | tf_op jit(solution)/shard_map/ppermute | solution.py:216
  41.3 2.3 %collective-permute-done.3 = f32[13,1024]{1,0:T(8,128)S(1)} collective-permute-done((f32[13,1024]{1,0:T(8,128)S(1)}, f32[13,1024]{1,0:T(8,128)S(1)}, u32[]{:S(2)}, u32[]{:S(2)}) %collective-permute-start.3) | collective-permute-done | bytes 53280 | tf_op jit(solution)/shard_map/ppermute | solution.py:216
  43.6 2.1 %collective-permute-start.4 = (f32[13,1024]{1,0:T(8,128)S(1)}, f32[13,1024]{1,0:T(8,128)S(1)}, u32[]{:S(2)}, u32[]{:S(2)}) collective-permute-start(f32[13,1024]{1,0:T(8,128)S(1)} %add.951), channel_id=1, source_target_pairs={{0,8},{2,10},{4,12},{6,14},{8,0},{10,2},{12,4},{14,6},{16,24},{18,... | collective-permute-start | bytes 159752 | tf_op jit(solution)/shard_map/ppermute | solution.py:216
  45.7 2.2 %collective-permute-done.4 = f32[13,1024]{1,0:T(8,128)S(1)} collective-permute-done((f32[13,1024]{1,0:T(8,128)S(1)}, f32[13,1024]{1,0:T(8,128)S(1)}, u32[]{:S(2)}, u32[]{:S(2)}) %collective-permute-start.4) | collective-permute-done | bytes 53280 | tf_op jit(solution)/shard_map/ppermute | solution.py:216
  47.9 3.7 %collective-permute-start.5 = (f32[13,1024]{1,0:T(8,128)S(1)}, f32[13,1024]{1,0:T(8,128)S(1)}, u32[]{:S(2)}, u32[]{:S(2)}) collective-permute-start(f32[13,1024]{1,0:T(8,128)S(1)} %add.952), channel_id=1, source_target_pairs={{0,16},{2,18},{4,20},{6,22},{8,24},{10,26},{12,28},{14,30},{16,0},... | collective-permute-start | bytes 159752 | tf_op jit(solution)/shard_map/ppermute | solution.py:216
  51.7 2.2 %collective-permute-done.5 = f32[13,1024]{1,0:T(8,128)S(1)} collective-permute-done((f32[13,1024]{1,0:T(8,128)S(1)}, f32[13,1024]{1,0:T(8,128)S(1)}, u32[]{:S(2)}, u32[]{:S(2)}) %collective-permute-start.5) | collective-permute-done | bytes 53280 | tf_op jit(solution)/shard_map/ppermute | solution.py:216
  54.1 0.5 collective-permute-start.7
  54.6 0.6 collective-permute-done.6
  55.2 0.2 collective-permute-done.7
  55.6 0.1 fusion.83
  55.8 0.1 fusion.79
  56.1 0.1 fusion.75
  56.5 4.6 %fusion.11 = f32[1024,8,128]{0,2,1:T(8,128)S(1)} fusion(f32[1024,8,128]{0,2,1:T(8,128)S(1)} %fusion.47, f32[8,128]{1,0:T(8,128)S(1)} %bitcast.117, f32[8,128]{1,0:T(8,128)S(1)} %bitcast.115, f32[8,128]{1,0:T(8,128)S(1)} %bitcast.114, f32[8,128]{1,0:T(8,128)S(1)} %fusion.113, f32[8,128]{1,0:T(8,128)S(1)} %bitcast.111, f32[8,128]{1,0:T(8,128)S(1)} %get-tuple-element.71, ...), kind=kLoop, calls=%fused_computation.23 | loop fusion | flops 28311552 | bytes 8451072 | tf_op jit(solution)/shard_map/jit(_where)/select_n | solution.py:185
  61.2 1.9 %copy-done = f32[1024,8,128]{0,2,1:T(8,128)} copy-done((f32[1024,8,128]{0,2,1:T(8,128)}, f32[1024,8,128]{0,2,1:T(8,128)S(1)}, u32[]{:S(2)}) %copy-start) | copy-done | bytes 4194328
  63.3 0.2 copy.34
  63.5 0.2 copy.36
  63.7 0.4 collective-permute-start.9
  64.1 0.2 collective-permute-start.8
  64.2 8.7 %fusion.172 = (f32[1024,8,127]{0,2,1:T(8,128)}, f32[1024,8,127]{0,2,1:T(8,128)}) fusion(f32[1024,8,128]{0,2,1:T(8,128)} %copy-done), kind=kLoop, calls=%fused_computation.286 | loop fusion | bytes 16646144 | tf_op jit(solution)/shard_map/jit(_roll_static)/slice | solution.py:118
  73.0 0.2 copy.37
  73.2 0.2 copy.35
  73.4 8.8 %fusion.40 = f32[1024,8,128]{0,2,1:T(8,128)S(1)} fusion(f32[1024,8,128]{0,2,1:T(8,128)} %copy-done, f32[1024,1,128]{0,2,1:T(8,128)S(1)} %copy.37, f32[1024,1,128]{0,2,1:T(8,128)S(1)} %copy.35, f32[1024,8,127]{0,2,1:T(8,128)} %get-tuple-element.11, f32[1024,8,1]{0,2,1:T(1,128)S(1)} %get-tuple-element.13, f32[1024,8,1]{0,2,1:T(1,128)S(1)} %get-tuple-element.12, ...), kind=kLoop, calls=%fused_computation.53 | loop fusion | flops 16777216 | bytes 17836032 | tf_op jit(solution)/shard_map/sub | solution.py:126
  82.2 3.6 %fusion.56 = f32[13,1024]{1,0:T(8,128)S(1)} fusion(f32[1024,1024]{0,1:T(8,128)S(1)} %bitcast.94, f32[13,1024]{1,0:T(8,128)S(1)} %stack.16), kind=kOutput, calls=%fused_computation.76 | convolution fusion | flops 163591168 | bytes 4300800 | tf_op jit(solution)/shard_map/dot_general | solution.py:207
  85.8 1.5 %collective-permute-start.10 = (f32[13,1024]{1,0:T(8,128)S(1)}, f32[13,1024]{1,0:T(8,128)S(1)}, u32[]{:S(2)}, u32[]{:S(2)}) collective-permute-start(f32[13,1024]{1,0:T(8,128)S(1)} %fusion.56), channel_id=1, source_target_pairs={{0,2},{2,0},{4,6},{6,4},{8,10},{10,8},{12,14},{14,12},{16,18},{18,... | collective-permute-start | bytes 159752 | tf_op jit(solution)/shard_map/ppermute | solution.py:216
  87.3 2.9 %collective-permute-done.10 = f32[13,1024]{1,0:T(8,128)S(1)} collective-permute-done((f32[13,1024]{1,0:T(8,128)S(1)}, f32[13,1024]{1,0:T(8,128)S(1)}, u32[]{:S(2)}, u32[]{:S(2)}) %collective-permute-start.10) | collective-permute-done | bytes 53280 | tf_op jit(solution)/shard_map/ppermute | solution.py:216
  90.1 1.6 %collective-permute-start.11 = (f32[13,1024]{1,0:T(8,128)S(1)}, f32[13,1024]{1,0:T(8,128)S(1)}, u32[]{:S(2)}, u32[]{:S(2)}) collective-permute-start(f32[13,1024]{1,0:T(8,128)S(1)} %add.995), channel_id=1, source_target_pairs={{0,4},{2,6},{4,0},{6,2},{8,12},{10,14},{12,8},{14,10},{16,20},{18,... | collective-permute-start | bytes 159752 | tf_op jit(solution)/shard_map/ppermute | solution.py:216
  91.7 2.7 %collective-permute-done.11 = f32[13,1024]{1,0:T(8,128)S(1)} collective-permute-done((f32[13,1024]{1,0:T(8,128)S(1)}, f32[13,1024]{1,0:T(8,128)S(1)}, u32[]{:S(2)}, u32[]{:S(2)}) %collective-permute-start.11) | collective-permute-done | bytes 53280 | tf_op jit(solution)/shard_map/ppermute | solution.py:216
  94.5 1.4 %collective-permute-start.12 = (f32[13,1024]{1,0:T(8,128)S(1)}, f32[13,1024]{1,0:T(8,128)S(1)}, u32[]{:S(2)}, u32[]{:S(2)}) collective-permute-start(f32[13,1024]{1,0:T(8,128)S(1)} %add.996), channel_id=1, source_target_pairs={{0,8},{2,10},{4,12},{6,14},{8,0},{10,2},{12,4},{14,6},{16,24},{18,... | collective-permute-start | bytes 159752 | tf_op jit(solution)/shard_map/ppermute | solution.py:216
  95.9 3.0 %collective-permute-done.12 = f32[13,1024]{1,0:T(8,128)S(1)} collective-permute-done((f32[13,1024]{1,0:T(8,128)S(1)}, f32[13,1024]{1,0:T(8,128)S(1)}, u32[]{:S(2)}, u32[]{:S(2)}) %collective-permute-start.12) | collective-permute-done | bytes 53280 | tf_op jit(solution)/shard_map/ppermute | solution.py:216
  98.8 3.4 %collective-permute-start.13 = (f32[13,1024]{1,0:T(8,128)S(1)}, f32[13,1024]{1,0:T(8,128)S(1)}, u32[]{:S(2)}, u32[]{:S(2)}) collective-permute-start(f32[13,1024]{1,0:T(8,128)S(1)} %add.997), channel_id=1, source_target_pairs={{0,16},{2,18},{4,20},{6,22},{8,24},{10,26},{12,28},{14,30},{16,0},... | collective-permute-start | bytes 159752 | tf_op jit(solution)/shard_map/ppermute | solution.py:216
  102.2 2.2 %collective-permute-done.13 = f32[13,1024]{1,0:T(8,128)S(1)} collective-permute-done((f32[13,1024]{1,0:T(8,128)S(1)}, f32[13,1024]{1,0:T(8,128)S(1)}, u32[]{:S(2)}, u32[]{:S(2)}) %collective-permute-start.13) | collective-permute-done | bytes 53280 | tf_op jit(solution)/shard_map/ppermute | solution.py:216
  104.7 0.5 collective-permute-start.15
  105.2 0.6 collective-permute-done.14
  105.8 0.2 collective-permute-done.15
  107.1 6.4 %fusion.29 = f32[1024,8,128]{0,2,1:T(8,128)} fusion(f32[1024,8,128]{0,2,1:T(8,128)S(1)} %fusion.40, f32[8,128]{1,0:T(8,128)S(1)} %bitcast.116, f32[8,128]{1,0:T(8,128)S(1)} %bitcast.113, f32[8,128]{1,0:T(8,128)S(1)} %bitcast.112, f32[8,128]{1,0:T(8,128)S(1)} %fusion.115, f32[8,128]{1,0:T(8,128)S(1)} %bitcast.110, f32[8,128]{1,0:T(8,128)S(1)} %get-tuple-element.68, ...), kind=kLoop, calls=%fused_computation.41 | loop fusion | flops 28311552 | bytes 8451072 | tf_op jit(solution)/shard_map/jit(_where)/select_n | solution.py:185
  113.5 5.4 %copy.38 = f32[1024,8,128]{2,1,0:T(8,128)} copy(f32[1024,8,128]{0,2,1:T(8,128)} %fusion.29) | data formatting | bytes 8388608
  (79 shorter events, 3.1 us)
Async XLA Ops:
  4.8 16.5 %collective-permute-start.1 = (f32[1024,1,128]{2,0,1:T(8,128)S(1)}, f32[1024,1,128]{2,0,1:T(8,128)S(1)}, u32[]{:S(2)}, u32[]{:S(2)}) collective-permute-start(f32[1024,1,128]{2,0,1:T(8,128)S(1)} %bitcast.97), channel_id=1, source_target_pairs={{1,0},{0,1},{3,2},{2,3},{5,4},{4,5},{7,6},{6,7},{9,8},{8,9},{11,10... | collective-permute-start | bytes 1572872 | tf_op jit(solution)/shard_map/ppermute | solution.py:26
  5.4 16.2 %collective-permute-start = (f32[1024,1,128]{2,0,1:T(8,128)S(1)}, f32[1024,1,128]{2,0,1:T(8,128)S(1)}, u32[]{:S(2)}, u32[]{:S(2)}) collective-permute-start(f32[1024,1,128]{2,0,1:T(8,128)S(1)} %bitcast.96), channel_id=1, source_target_pairs={{0,1},{1,0},{2,3},{3,2},{4,5},{5,4},{6,7},{7,6},{8,9},{9,8},{10,11... | collective-permute-start | bytes 1572872 | tf_op jit(solution)/shard_map/ppermute | solution.py:25
  30.4 15.3 %copy-start.3 = (s32[8,128]{1,0:T(8,128)S(1)}, s32[8,128]{1,0:T(8,128)}, u32[]{:S(2)}) copy-start(s32[8,128]{1,0:T(8,128)} %param.5) | copy-start | bytes 12292
  30.4 26.1 %copy-start.2 = (s32[8,128]{1,0:T(8,128)S(1)}, s32[8,128]{1,0:T(8,128)}, u32[]{:S(2)}) copy-start(s32[8,128]{1,0:T(8,128)} %param.4) | copy-start | bytes 12292
  34.0 5.3 %collective-permute-start.2 = (f32[13,1024]{1,0:T(8,128)S(1)}, f32[13,1024]{1,0:T(8,128)S(1)}, u32[]{:S(2)}, u32[]{:S(2)}) collective-permute-start(f32[13,1024]{1,0:T(8,128)S(1)} %fusion.58), channel_id=1, source_target_pairs={{0,2},{2,0},{4,6},{6,4},{8,10},{10,8},{12,14},{14,12},{16,18},{18,... | collective-permute-start | bytes 159752 | tf_op jit(solution)/shard_map/ppermute | solution.py:216
  39.3 4.3 %collective-permute-start.3 = (f32[13,1024]{1,0:T(8,128)S(1)}, f32[13,1024]{1,0:T(8,128)S(1)}, u32[]{:S(2)}, u32[]{:S(2)}) collective-permute-start(f32[13,1024]{1,0:T(8,128)S(1)} %add.950), channel_id=1, source_target_pairs={{0,4},{2,6},{4,0},{6,2},{8,12},{10,14},{12,8},{14,10},{16,20},{18,... | collective-permute-start | bytes 159752 | tf_op jit(solution)/shard_map/ppermute | solution.py:216
  43.6 4.3 %collective-permute-start.4 = (f32[13,1024]{1,0:T(8,128)S(1)}, f32[13,1024]{1,0:T(8,128)S(1)}, u32[]{:S(2)}, u32[]{:S(2)}) collective-permute-start(f32[13,1024]{1,0:T(8,128)S(1)} %add.951), channel_id=1, source_target_pairs={{0,8},{2,10},{4,12},{6,14},{8,0},{10,2},{12,4},{14,6},{16,24},{18,... | collective-permute-start | bytes 159752 | tf_op jit(solution)/shard_map/ppermute | solution.py:216
  47.9 5.9 %collective-permute-start.5 = (f32[13,1024]{1,0:T(8,128)S(1)}, f32[13,1024]{1,0:T(8,128)S(1)}, u32[]{:S(2)}, u32[]{:S(2)}) collective-permute-start(f32[13,1024]{1,0:T(8,128)S(1)} %add.952), channel_id=1, source_target_pairs={{0,16},{2,18},{4,20},{6,22},{8,24},{10,26},{12,28},{14,30},{16,0},... | collective-permute-start | bytes 159752 | tf_op jit(solution)/shard_map/ppermute | solution.py:216
  54.0 1.2 %collective-permute-start.6 = (f32[5,4,128]{2,1,0:T(4,128)S(1)}, f32[5,4,128]{2,1,0:T(4,128)S(1)}, u32[]{:S(2)}, u32[]{:S(2)}) collective-permute-start(f32[5,4,128]{2,1,0:T(4,128)S(1)} %get-tuple-element.64), channel_id=1, source_target_pairs={{0,1},{1,0},{2,3},{3,2},{4,5},{5,4},{6,7},{7,6},{8,9},{9,8},{10,11... | collective-permute-start | bytes 30728 | tf_op jit(solution)/shard_map/ppermute | solution.py:25
  54.1 1.3 %collective-permute-start.7 = (f32[5,4,128]{2,1,0:T(4,128)S(1)}, f32[5,4,128]{2,1,0:T(4,128)S(1)}, u32[]{:S(2)}, u32[]{:S(2)}) collective-permute-start(f32[5,4,128]{2,1,0:T(4,128)S(1)} %get-tuple-element.65), channel_id=1, source_target_pairs={{1,0},{0,1},{3,2},{2,3},{5,4},{4,5},{7,6},{6,7},{9,8},{8,9},{11,10... | collective-permute-start | bytes 30728 | tf_op jit(solution)/shard_map/ppermute | solution.py:26
  61.2 2.0 %copy-start = (f32[1024,8,128]{0,2,1:T(8,128)}, f32[1024,8,128]{0,2,1:T(8,128)S(1)}, u32[]{:S(2)}) copy-start(f32[1024,8,128]{0,2,1:T(8,128)S(1)} %fusion.11) | copy-start | bytes 12582916
  63.7 9.3 %collective-permute-start.9 = (f32[1024,1,128]{2,0,1:T(8,128)S(1)}, f32[1024,1,128]{2,0,1:T(8,128)S(1)}, u32[]{:S(2)}, u32[]{:S(2)}) collective-permute-start(f32[1024,1,128]{2,0,1:T(8,128)S(1)} %copy.36), channel_id=1, source_target_pairs={{1,0},{0,1},{3,2},{2,3},{5,4},{4,5},{7,6},{6,7},{9,8},{8,9},{11,10... | collective-permute-start | bytes 1572872 | tf_op jit(solution)/shard_map/ppermute | solution.py:26
  64.1 9.1 %collective-permute-start.8 = (f32[1024,1,128]{2,0,1:T(8,128)S(1)}, f32[1024,1,128]{2,0,1:T(8,128)S(1)}, u32[]{:S(2)}, u32[]{:S(2)}) collective-permute-start(f32[1024,1,128]{2,0,1:T(8,128)S(1)} %copy.34), channel_id=1, source_target_pairs={{0,1},{1,0},{2,3},{3,2},{4,5},{5,4},{6,7},{7,6},{8,9},{9,8},{10,11... | collective-permute-start | bytes 1572872 | tf_op jit(solution)/shard_map/ppermute | solution.py:25
  85.8 4.4 %collective-permute-start.10 = (f32[13,1024]{1,0:T(8,128)S(1)}, f32[13,1024]{1,0:T(8,128)S(1)}, u32[]{:S(2)}, u32[]{:S(2)}) collective-permute-start(f32[13,1024]{1,0:T(8,128)S(1)} %fusion.56), channel_id=1, source_target_pairs={{0,2},{2,0},{4,6},{6,4},{8,10},{10,8},{12,14},{14,12},{16,18},{18,... | collective-permute-start | bytes 159752 | tf_op jit(solution)/shard_map/ppermute | solution.py:216
  90.1 4.3 %collective-permute-start.11 = (f32[13,1024]{1,0:T(8,128)S(1)}, f32[13,1024]{1,0:T(8,128)S(1)}, u32[]{:S(2)}, u32[]{:S(2)}) collective-permute-start(f32[13,1024]{1,0:T(8,128)S(1)} %add.995), channel_id=1, source_target_pairs={{0,4},{2,6},{4,0},{6,2},{8,12},{10,14},{12,8},{14,10},{16,20},{18,... | collective-permute-start | bytes 159752 | tf_op jit(solution)/shard_map/ppermute | solution.py:216
  94.5 4.3 %collective-permute-start.12 = (f32[13,1024]{1,0:T(8,128)S(1)}, f32[13,1024]{1,0:T(8,128)S(1)}, u32[]{:S(2)}, u32[]{:S(2)}) collective-permute-start(f32[13,1024]{1,0:T(8,128)S(1)} %add.996), channel_id=1, source_target_pairs={{0,8},{2,10},{4,12},{6,14},{8,0},{10,2},{12,4},{14,6},{16,24},{18,... | collective-permute-start | bytes 159752 | tf_op jit(solution)/shard_map/ppermute | solution.py:216
  98.8 5.6 %collective-permute-start.13 = (f32[13,1024]{1,0:T(8,128)S(1)}, f32[13,1024]{1,0:T(8,128)S(1)}, u32[]{:S(2)}, u32[]{:S(2)}) collective-permute-start(f32[13,1024]{1,0:T(8,128)S(1)} %add.997), channel_id=1, source_target_pairs={{0,16},{2,18},{4,20},{6,22},{8,24},{10,26},{12,28},{14,30},{16,0},... | collective-permute-start | bytes 159752 | tf_op jit(solution)/shard_map/ppermute | solution.py:216
  104.6 1.2 %collective-permute-start.14 = (f32[5,4,128]{2,1,0:T(4,128)S(1)}, f32[5,4,128]{2,1,0:T(4,128)S(1)}, u32[]{:S(2)}, u32[]{:S(2)}) collective-permute-start(f32[5,4,128]{2,1,0:T(4,128)S(1)} %get-tuple-element.62), channel_id=1, source_target_pairs={{0,1},{1,0},{2,3},{3,2},{4,5},{5,4},{6,7},{7,6},{8,9},{9,8},{10,11... | collective-permute-start | bytes 30728 | tf_op jit(solution)/shard_map/ppermute | solution.py:25
  104.7 1.3 %collective-permute-start.15 = (f32[5,4,128]{2,1,0:T(4,128)S(1)}, f32[5,4,128]{2,1,0:T(4,128)S(1)}, u32[]{:S(2)}, u32[]{:S(2)}) collective-permute-start(f32[5,4,128]{2,1,0:T(4,128)S(1)} %get-tuple-element.63), channel_id=1, source_target_pairs={{1,0},{0,1},{3,2},{2,3},{5,4},{4,5},{7,6},{6,7},{9,8},{8,9},{11,10... | collective-permute-start | bytes 30728 | tf_op jit(solution)/shard_map/ppermute | solution.py:26
  107.0 6.5 %copy-start.1 = (f32[5,8,128]{2,1,0:T(8,128)}, f32[5,8,128]{2,1,0:T(8,128)S(1)}, u32[]{:S(2)}) copy-start(f32[5,8,128]{2,1,0:T(8,128)S(1)} %fusion.87) | copy-start | bytes 61444
